TPU v7x, 32 devices: a whole 2x2x4 slice. The times are simulated.
32 devices in a mesh: seq: 16 (over z, y, core), head: 2 (over x).
Axes of the slice: x: 2, y: 2, z: 4, core: 2. Of those that a mesh axis runs over, the one named last changes fastest.
Arguments:
- qkv: bfloat16 [3, 2048, 1024], P(None, ('seq', 'head')), may hold values from -128 to 128
- token_rate: float32 [2048, 2], P('seq', 'head'), may hold values from 0.1 to 1
- head_rate: float32 [2], P('head'), may hold values from 0.5 to 2
- fast_state: float32 [3, 2, 512, 512], P(None, 'head', 'seq'), may hold values from -0.25 to 0.25
Outputs:
- combined: bfloat16 [2048, 1024], P(('seq', 'head'))
- new_state: float32 [3, 2, 512, 512], P(None, 'head', 'seq')
All inputs are finite; a program needn't handle non-finite values.
Results may differ from a plain program's by a relative error of at most 0.017.
Values may be sent and summed in bfloat16 or wider, within the bound.
A program may use at most 64 MiB of HBM per device.

v0:
```python
import jax
import jax.numpy as jnp
from jax import lax
from jax.sharding import PartitionSpec as P

WINDOW = 1024
NS_STEPS = 2


ns_first = 3.4445
ns_second = -4.775
ns_third = 2.0315
rms_eps = 1e-06
norm_eps = 1e-07
precise = lax.Precision.HIGHEST


def from_behind(block, axis, distance):
    devices = range(lax.axis_size(axis))
    route = [(i - distance, i) for i in devices if i - distance in devices]
    return lax.ppermute(block, axis, route)


def rms_scaled(values):
    return values * lax.rsqrt(jnp.mean(values * values, axis=-1, keepdims=True) + rms_eps)


def contract_last(left_side, right_side):
    return lax.dot_general(
        left_side, right_side, (((1,), (1,)), ((), ())), preferred_element_type=jnp.float32
    )


def contract_first(left_side, right_side):
    return lax.dot_general(
        left_side, right_side, (((0,), (0,)), ((), ())), preferred_element_type=jnp.float32
    )


def head_gradient(key_norm, signal, weight_piece):
    gate_act = contract_last(key_norm, weight_piece[0])
    up_act = contract_last(key_norm, weight_piece[1])
    active = (jax.nn.silu(gate_act) * up_act).astype(jnp.bfloat16)
    back_grad = contract_last(signal, weight_piece[2])
    sigmoid_gate = jax.nn.sigmoid(gate_act)
    grad_gate = (
        back_grad * up_act * sigmoid_gate * (1.0 + gate_act * (1.0 - sigmoid_gate))
    ).astype(jnp.bfloat16)
    grad_up = (back_grad * jax.nn.silu(gate_act)).astype(jnp.bfloat16)
    return jnp.stack(
        [
            contract_first(grad_gate, key_norm),
            contract_first(grad_up, key_norm),
            contract_first(active, signal),
        ]
    )


def gram_times(gram_matrix, section_number, row_block):
    if section_number == 0:
        return jnp.einsum("mij,mjk->mik", row_block, gram_matrix, precision=precise)
    once_moved = gram_times(gram_matrix, section_number - 1, row_block)
    return poly_times(
        gram_matrix, section_number - 1, poly_times(gram_matrix, section_number - 1, once_moved)
    )


def poly_times(gram_matrix, section_number, row_block):
    moved_once = gram_times(gram_matrix, section_number, row_block)
    moved_twice = gram_times(gram_matrix, section_number, moved_once)
    return ns_first * row_block + ns_second * moved_once + ns_third * moved_twice


def shards(qkv, token_rate, head_rate, fast_state):
    grouped = lax.all_to_all(qkv, "head", split_axis=2, concat_axis=1, tiled=True)
    tok_rows = grouped.shape[1]
    head_dim = grouped.shape[2]
    seq_index = lax.axis_index("seq")
    state_rows = fast_state.shape[2]
    query_norm = rms_scaled(grouped[0].astype(jnp.float32)).astype(jnp.bfloat16)
    key_norm = rms_scaled(grouped[1].astype(jnp.float32)).astype(jnp.bfloat16)
    signal = (-token_rate * grouped[2].astype(jnp.float32)).astype(jnp.bfloat16)
    old_state = fast_state[:, 0]
    old_low = old_state.astype(jnp.bfloat16)
    partial_value = head_gradient(
        key_norm, signal, lax.all_gather(old_low, "seq", axis=1, tiled=True)
    )
    summed = lax.psum(partial_value, "seq")
    frob_norm = jnp.sqrt(jnp.sum(summed * summed, axis=(1, 2), keepdims=True))
    normalized = summed / (frob_norm + norm_eps)
    gram_matrix = jnp.einsum("mij,mkj->mik", normalized, normalized, precision=precise)
    hidden_units = gram_matrix.shape[1]
    selector = (
        jnp.arange(hidden_units, dtype=jnp.int32)[None, :]
        == seq_index * state_rows + jnp.arange(state_rows, dtype=jnp.int32)[:, None]
    ).astype(jnp.float32)
    row_block = jnp.broadcast_to(selector, (3, state_rows, hidden_units))
    for section_number in range(NS_STEPS - 1, -1, -1):
        row_block = poly_times(gram_matrix, section_number, row_block)
    final_rows = jnp.einsum("mij,mjk->mik", row_block, normalized, precision=precise)
    new_rows = old_state - head_rate[0] * final_rows
    weight_piece = lax.all_gather(new_rows.astype(jnp.bfloat16), "seq", axis=1, tiled=True)
    gate_act = contract_last(query_norm, weight_piece[0])
    up_act = contract_last(query_norm, weight_piece[1])
    active = (jax.nn.silu(gate_act) * up_act).astype(jnp.bfloat16)
    fast_out = jnp.dot(active, weight_piece[2], preferred_element_type=jnp.float32)
    key_value = grouped[1:3]
    reach_blocks = WINDOW // tok_rows
    earlier = [from_behind(key_value, "seq", distance) for distance in range(reach_blocks, 0, -1)]
    context = jnp.concatenate(earlier + [key_value], axis=1)
    scores = contract_last(grouped[0], context[0]) * head_dim ** (-0.5)
    query_pos = seq_index * tok_rows + jnp.arange(tok_rows, dtype=jnp.int32)[:, None]
    key_pos = (
        seq_index * tok_rows - WINDOW + jnp.arange(WINDOW + tok_rows, dtype=jnp.int32)[None, :]
    )
    visible = (key_pos <= query_pos) & (key_pos > query_pos - WINDOW) & (key_pos >= 0)
    scores = jnp.where(visible, scores, -jnp.inf)
    row_max = jnp.max(scores, axis=1, keepdims=True)
    exp_scores = jnp.exp(scores - row_max)
    weights = (exp_scores / jnp.sum(exp_scores, axis=1, keepdims=True)).astype(jnp.bfloat16)
    attention = jnp.dot(weights, context[1], preferred_element_type=jnp.float32)
    combined = (attention + fast_out).astype(jnp.bfloat16)
    tokens_back = lax.all_to_all(combined, "head", split_axis=0, concat_axis=1, tiled=True)
    return (tokens_back, new_rows[:, None])


def solution(mesh):
    return jax.shard_map(
        shards,
        mesh=mesh,
        in_specs=(
            P(None, ("seq", "head"), None),
            P("seq", "head"),
            P("head"),
            P(None, "head", "seq", None),
        ),
        out_specs=(P(("seq", "head"), None), P(None, "head", "seq", None)),
        check_vma=False,
    )
```

profile of v0, /device:TPU:16, one launch (start us, length us, event | category | flops | bytes accessed | tf_op | source)
XLA Modules:
  0.0 289.8 jit_solution(17737878514424476235)
XLA Ops:
  7.2 0.0 all-gather.3.cloned.1.call-start
  7.2 1.6 bitcast_convert_fusion
  8.8 1.6 copy.38
  10.4 1.4 reshape.124
  11.9 3.5 %all-to-all-start = ((bf16[2,2,49152]{2,1,0:T(2,128)(2,1)}), bf16[2,2,49152]{2,1,0:T(2,128)(2,1)S(1)}, u32[]{:S(2)}, u32[]{:S(2)}) async-start(bf16[2,2,49152]{2,1,0:T(2,128)(2,1)} %reshape.124), calls=%async_computation | async-start | bytes 786432 | tf_op jit(solution)/shard_map/all_to_all | solution.py:75
  15.3 0.0 all-reduce.2.cloned.1.call-start
  15.4 0.1 mul.168
  15.5 6.7 %all-to-all-done = bf16[2,2,49152]{2,1,0:T(2,128)(2,1)S(1)} async-done(((bf16[2,2,49152]{2,1,0:T(2,128)(2,1)}), bf16[2,2,49152]{2,1,0:T(2,128)(2,1)S(1)}, u32[]{:S(2)}, u32[]{:S(2)}) %all-to-all-start) | async-done | bytes 393248 | tf_op jit(solution)/shard_map/all_to_all | solution.py:75
  22.2 0.6 reshape.125
  22.8 0.6 copy.40
  23.4 0.1 multiply_reduce_fusion.1
  23.5 0.1 rsqrt.22
  23.7 0.1 fusion.25
  23.7 0.1 fusion.26
  23.8 0.1 multiply_convert_fusion.4
  24.0 25.6 %all-gather.3.cloned.1.call-done = bf16[3,512,512]{2,1,0:T(8,128)(2,1)} async-done(((bf16[3,32,512]{2,1,0:T(8,128)(2,1)}), bf16[3,512,512]{2,1,0:T(8,128)(2,1)}) %all-gather.3.cloned.1.call-update) | async-done | bytes 1572880 | tf_op jit(solution)/shard_map/all_gather | solution.py:86
  49.6 1.3 fusion.17
  51.0 1.3 fusion.19
  52.3 0.3 convolution_bitcast_fusion.1
  52.7 1.3 fusion.18
  54.0 0.3 convolution_bitcast_fusion.2
  54.4 0.3 convolution_bitcast_fusion
  54.7 2.0 pad_maximum_fusion
  56.7 0.2 all-gather.5.cloned.1.call-start
  57.6 0.1 fusion.37
  57.7 0.1 fusion.38
  57.8 102.6 %all-reduce.2.cloned.1.call-done = f32[3,512,512]{2,1,0:T(8,128)} async-done(((f32[3,512,512]{2,1,0:T(8,128)}), f32[3,512,512]{2,1,0:T(8,128)}) %all-reduce.2.cloned.1.call-update) | async-done | bytes 3145744 | tf_op jit(solution)/shard_map/psum | solution.py:88
  160.3 2.5 multiply_reduce_fusion
  162.8 0.4 copy-done
  163.2 5.6 %fusion.15 = f32[3,512,512]{2,1,0:T(8,128)S(1)} fusion(f32[3,512,512]{2,1,0:T(8,128)S(1)} %copy-done, f32[3]{0:T(128)S(1)} %sqrt_add_fusion), kind=kOutput, calls=%fused_computation.33 | convolution fusion | flops 4832624640 | bytes 6291468 | tf_op jit(solution)/shard_map/mij,mkj->mik/dot_general | solution.py:91
  168.8 1.9 fusion.35
  170.7 1.9 fusion.48
  172.6 1.9 fusion.12
  174.5 1.9 fusion.49
  176.4 2.1 fusion.11
  178.5 1.9 fusion.50
  180.4 1.9 fusion.51
  182.3 1.9 fusion.10
  184.3 1.9 fusion.52
  186.2 1.9 fusion.9
  188.1 1.9 fusion.53
  190.0 2.1 fusion.6
  192.1 2.8 fusion.46
  195.0 1.3 collective-permute-start
  196.3 1.9 collective-permute-start.1
  198.2 2.9 collective-permute-start.2
  201.1 1.9 collective-permute-start.3
  203.1 1.9 collective-permute-start.4
  205.0 2.3 collective-permute-done
  207.3 1.9 collective-permute-start.5
  209.2 12.2 %collective-permute-start.6 = (bf16[2,128,512]{2,1,0:T(8,128)(2,1)S(1)}, bf16[2,128,512]{2,1,0:T(8,128)(2,1)S(1)}, u32[]{:S(2)}, u32[]{:S(2)}) collective-permute-start(bf16[2,128,512]{2,1,0:T(8,128)(2,1)S(1)} %bitcast.119), channel_id=1, source_target_pairs={{0,4},{2,6},{4,8},{6,10},{8,12},{10,14},{12,16},{14,18},{16,20},{1... | collective-permute-start | bytes 786440 | tf_op jit(solution)/shard_map/ppermute | solution.py:21
  221.5 0.4 collective-permute-done.2
  221.8 13.3 %collective-permute-start.7 = (bf16[2,128,512]{2,1,0:T(8,128)(2,1)S(1)}, bf16[2,128,512]{2,1,0:T(8,128)(2,1)S(1)}, u32[]{:S(2)}, u32[]{:S(2)}) collective-permute-start(bf16[2,128,512]{2,1,0:T(8,128)(2,1)S(1)} %bitcast.120), channel_id=1, source_target_pairs={{0,2},{2,4},{4,6},{6,8},{8,10},{10,12},{12,14},{14,16},{16,18},{18... | collective-permute-start | bytes 786440 | tf_op jit(solution)/shard_map/ppermute | solution.py:21
  235.2 8.6 %collective-permute-done.4 = bf16[2,128,512]{2,1,0:T(8,128)(2,1)S(1)} collective-permute-done((bf16[2,128,512]{2,1,0:T(8,128)(2,1)S(1)}, bf16[2,128,512]{2,1,0:T(8,128)(2,1)S(1)}, u32[]{:S(2)}, u32[]{:S(2)}) %collective-permute-start.4) | collective-permute-done | bytes 262176 | tf_op jit(solution)/shard_map/ppermute | solution.py:21
  243.9 2.9 collective-permute-done.5
  246.8 20.7 %collective-permute-done.6 = bf16[2,128,512]{2,1,0:T(8,128)(2,1)S(1)} collective-permute-done((bf16[2,128,512]{2,1,0:T(8,128)(2,1)S(1)}, bf16[2,128,512]{2,1,0:T(8,128)(2,1)S(1)}, u32[]{:S(2)}, u32[]{:S(2)}) %collective-permute-start.6) | collective-permute-done | bytes 262176 | tf_op jit(solution)/shard_map/ppermute | solution.py:21
  267.5 2.3 collective-permute-done.7
  269.9 0.5 fusion.47
  270.4 0.2 fusion.20
  270.6 1.3 fusion.16
  271.9 2.4 fusion.14
  274.3 1.3 fusion.13
  275.6 7.0 %all_to_all.34 = bf16[2,64,512]{2,1,0:T(8,128)(2,1)S(1)} all-to-all(bf16[2,64,512]{2,1,0:T(8,128)(2,1)S(1)} %bitcast.127), channel_id=1, replica_groups=mesh['seq'=16,'head'=2] {'head'}, dimensions={0} | all-to-all | bytes 262144 | tf_op jit(solution)/shard_map/all_to_all | solution.py:123
  282.6 0.7 copy.51
  (29 shorter events, 0.4 us)
Async XLA Ops:
  7.2 8.2 %copy-start.2 = (f32[128,1]{0,1:T(1,128)S(1)}, f32[128,1]{0,1:T(1,128)}, u32[]{:S(2)}) copy-start(f32[128,1]{0,1:T(1,128)} %param.5) | copy-start | bytes 1540
  7.2 42.5 %all-gather.3.cloned.1.call-start = ((), (), s32[]{:S(2)}) async-start(), calls=%async_computation.2 | async-start | bytes 1671168 | tf_op jit(solution)/shard_map/all_gather | solution.py:86
  11.9 10.3 %all-to-all-start = ((bf16[2,2,49152]{2,1,0:T(2,128)(2,1)}), bf16[2,2,49152]{2,1,0:T(2,128)(2,1)S(1)}, u32[]{:S(2)}, u32[]{:S(2)}) async-start(bf16[2,2,49152]{2,1,0:T(2,128)(2,1)} %reshape.124), calls=%async_computation | async-start | bytes 786432 | tf_op jit(solution)/shard_map/all_to_all | solution.py:75
  15.3 145.0 %all-reduce.2.cloned.1.call-start = ((), (), s32[]{:S(2)}) async-start(), calls=%async_computation.3 | async-start | bytes 6291456 | tf_op jit(solution)/shard_map/psum | solution.py:88
  56.7 213.8 %all-gather.5.cloned.1.call-start = ((), (), s32[]{:S(2)}) async-start(), calls=%async_computation.4 | async-start | bytes 1671168 | tf_op jit(solution)/shard_map/all_gather | solution.py:102
  160.3 2.8 copy-start
  188.1 4.1 %copy-start.1 = (f32[3,1,32,512]{3,2,1,0:T(8,128)S(1)}, f32[3,1,32,512]{3,2,1,0:T(8,128)}, u32[]{:S(2)}) copy-start(f32[3,1,32,512]{3,2,1,0:T(8,128)} %param.7) | copy-start | bytes 589828
  195.0 12.3 %collective-permute-start = (bf16[2,128,512]{2,1,0:T(8,128)(2,1)S(1)}, bf16[2,128,512]{2,1,0:T(8,128)(2,1)S(1)}, u32[]{:S(2)}, u32[]{:S(2)}) collective-permute-start(bf16[2,128,512]{2,1,0:T(8,128)(2,1)S(1)} %bitcast.113), channel_id=1, source_target_pairs={{0,16},{2,18},{4,20},{6,22},{8,24},{10,26},{12,28},{14,30},{1,17},... | collective-permute-start | bytes 786440 | tf_op jit(solution)/shard_map/ppermute | solution.py:21
  196.3 12.9 %collective-permute-start.1 = (bf16[2,128,512]{2,1,0:T(8,128)(2,1)S(1)}, bf16[2,128,512]{2,1,0:T(8,128)(2,1)S(1)}, u32[]{:S(2)}, u32[]{:S(2)}) collective-permute-start(bf16[2,128,512]{2,1,0:T(8,128)(2,1)S(1)} %bitcast.114), channel_id=1, source_target_pairs={{0,14},{2,16},{4,18},{6,20},{8,22},{10,24},{12,26},{14,28},{16,30}... | collective-permute-start | bytes 786440 | tf_op jit(solution)/shard_map/ppermute | solution.py:21
  198.2 23.6 %collective-permute-start.2 = (bf16[2,128,512]{2,1,0:T(8,128)(2,1)S(1)}, bf16[2,128,512]{2,1,0:T(8,128)(2,1)S(1)}, u32[]{:S(2)}, u32[]{:S(2)}) collective-permute-start(bf16[2,128,512]{2,1,0:T(8,128)(2,1)S(1)} %bitcast.115), channel_id=1, source_target_pairs={{0,12},{2,14},{4,16},{6,18},{8,20},{10,22},{12,24},{14,26},{16,28}... | collective-permute-start | bytes 786440 | tf_op jit(solution)/shard_map/ppermute | solution.py:21
  201.1 34.1 %collective-permute-start.3 = (bf16[2,128,512]{2,1,0:T(8,128)(2,1)S(1)}, bf16[2,128,512]{2,1,0:T(8,128)(2,1)S(1)}, u32[]{:S(2)}, u32[]{:S(2)}) collective-permute-start(bf16[2,128,512]{2,1,0:T(8,128)(2,1)S(1)} %bitcast.116), channel_id=1, source_target_pairs={{0,10},{2,12},{4,14},{6,16},{8,18},{10,20},{12,22},{14,24},{16,26}... | collective-permute-start | bytes 786440 | tf_op jit(solution)/shard_map/ppermute | solution.py:21
  203.1 40.8 %collective-permute-start.4 = (bf16[2,128,512]{2,1,0:T(8,128)(2,1)S(1)}, bf16[2,128,512]{2,1,0:T(8,128)(2,1)S(1)}, u32[]{:S(2)}, u32[]{:S(2)}) collective-permute-start(bf16[2,128,512]{2,1,0:T(8,128)(2,1)S(1)} %bitcast.117), channel_id=1, source_target_pairs={{0,8},{2,10},{4,12},{6,14},{8,16},{10,18},{12,20},{14,22},{16,24},... | collective-permute-start | bytes 786440 | tf_op jit(solution)/shard_map/ppermute | solution.py:21
  207.3 39.5 %collective-permute-start.5 = (bf16[2,128,512]{2,1,0:T(8,128)(2,1)S(1)}, bf16[2,128,512]{2,1,0:T(8,128)(2,1)S(1)}, u32[]{:S(2)}, u32[]{:S(2)}) collective-permute-start(bf16[2,128,512]{2,1,0:T(8,128)(2,1)S(1)} %bitcast.118), channel_id=1, source_target_pairs={{0,6},{2,8},{4,10},{6,12},{8,14},{10,16},{12,18},{14,20},{16,22},{... | collective-permute-start | bytes 786440 | tf_op jit(solution)/shard_map/ppermute | solution.py:21
  209.2 58.3 %collective-permute-start.6 = (bf16[2,128,512]{2,1,0:T(8,128)(2,1)S(1)}, bf16[2,128,512]{2,1,0:T(8,128)(2,1)S(1)}, u32[]{:S(2)}, u32[]{:S(2)}) collective-permute-start(bf16[2,128,512]{2,1,0:T(8,128)(2,1)S(1)} %bitcast.119), channel_id=1, source_target_pairs={{0,4},{2,6},{4,8},{6,10},{8,12},{10,14},{12,16},{14,18},{16,20},{1... | collective-permute-start | bytes 786440 | tf_op jit(solution)/shard_map/ppermute | solution.py:21
  221.8 48.0 %collective-permute-start.7 = (bf16[2,128,512]{2,1,0:T(8,128)(2,1)S(1)}, bf16[2,128,512]{2,1,0:T(8,128)(2,1)S(1)}, u32[]{:S(2)}, u32[]{:S(2)}) collective-permute-start(bf16[2,128,512]{2,1,0:T(8,128)(2,1)S(1)} %bitcast.120), channel_id=1, source_target_pairs={{0,2},{2,4},{4,6},{6,8},{8,10},{10,12},{12,14},{14,16},{16,18},{18... | collective-permute-start | bytes 786440 | tf_op jit(solution)/shard_map/ppermute | solution.py:21
Sparse Core Ops, SparseCore 0:
  10.7 38.8 all-gather.2
  56.8 103.4 all-reduce.1
  195.1 53.1 all-gather.4
where the time goes:
time: 290 us
  waiting for transfers between devices  172 us (59%)
  matrix products  42.2 us (15%)
  starting transfers between devices  41.2 us (14%)
  between operations  14.8 us (5%)
  blocking collectives  7 us (2%)
  other arithmetic  6.92 us (2%)
  local copies, waits for them, and re-layouts  5.59 us (2%)
    psum x1, waiting for transfers between devices, shards(): summed = lax.psum(partial_value, 'seq')  103 us
    ppermute x8, starting transfers between devices, from_behind(): return lax.ppermute(block, axis, route)  37.4 us
    ppermute x8, waiting for transfers between devices, from_behind(): return lax.ppermute(block, axis, route)  37.1 us
    all_gather x1, waiting for transfers between devices, shards(): lax.all_gather(old_low, 'seq', axis=1, tiled=True)  25.6 us
    dot_general x12, matrix products, gram_times(): return jnp.einsum('mij,mjk->mik', row_block, gram_matrix, precision=precise)  23.2 us
    all_to_all x1, blocking collectives, shards(): lax.all_to_all(combined, 'head', split_axis=0, concat_axis=1, tiled=True)  7 us
    all_to_all x1, waiting for transfers between devices, shards(): lax.all_to_all(qkv, 'head', split_axis=2, concat_axis=1, tiled=True)  6.67 us
    dot_general x5, matrix products, contract_last(): lax.dot_general(left_side, right_side, (((1,), (1,)), ((), ())), preferre...  5.86 us
  transfers between devices with their start and end apart: 12, of which 9 were waited for; matrix products, arithmetic and copies ran while one was open for 2% of the time, Pallas kernels for 0%

commit v1 on v0

v1 whole, which is shorter than its diff:
```python
import jax
import jax.numpy as jnp
from jax import lax
from jax.sharding import PartitionSpec as P

WINDOW = 1024
NS_STEPS = 2


ns_first = 3.4445
ns_second = -4.775
ns_third = 2.0315
rms_eps = 1e-06
norm_eps = 1e-07


def rms_scaled(values):
    return values * lax.rsqrt(jnp.mean(values * values, axis=-1, keepdims=True) + rms_eps)


def contract_last(left_side, right_side):
    return lax.dot_general(
        left_side, right_side, (((1,), (1,)), ((), ())), preferred_element_type=jnp.float32
    )


def contract_first(left_side, right_side):
    return lax.dot_general(
        left_side, right_side, (((0,), (0,)), ((), ())), preferred_element_type=jnp.float32
    )


def row_gradient(key_norm, signal, weight_rows):
    gate_act = contract_last(key_norm, weight_rows[0])
    up_act = contract_last(key_norm, weight_rows[1])
    back_grad = contract_last(signal, weight_rows[2])
    sigmoid_gate = jax.nn.sigmoid(gate_act)
    silu_gate = gate_act * sigmoid_gate
    active = (silu_gate * up_act).astype(jnp.bfloat16)
    grad_gate = (
        back_grad * up_act * sigmoid_gate * (1.0 + gate_act * (1.0 - sigmoid_gate))
    ).astype(jnp.bfloat16)
    grad_up = (back_grad * silu_gate).astype(jnp.bfloat16)
    return jnp.stack(
        [
            contract_first(grad_gate, key_norm),
            contract_first(grad_up, key_norm),
            contract_first(active, signal),
        ]
    )


def low_dot(left_side, right_side, subscripts):
    return jnp.einsum(
        subscripts,
        left_side.astype(jnp.bfloat16),
        right_side.astype(jnp.bfloat16),
        preferred_element_type=jnp.float32,
    )


def newton_schulz(gradients):
    frob_norm = jnp.sqrt(jnp.sum(gradients * gradients, axis=(1, 2), keepdims=True))
    iterate = gradients / (frob_norm + norm_eps)
    for _ in range(NS_STEPS):
        gram = low_dot(iterate, iterate, "mij,mkj->mik")
        poly = ns_second * gram + ns_third * low_dot(gram, gram, "mij,mjk->mik")
        iterate = ns_first * iterate + low_dot(poly, iterate, "mij,mjk->mik")
    return iterate


def shards(qkv, token_rate, head_rate, fast_state):
    grouped = lax.all_to_all(qkv, "head", split_axis=2, concat_axis=1, tiled=True)
    tok_rows = grouped.shape[1]
    head_dim = grouped.shape[2]
    seq_index = lax.axis_index("seq")
    state_rows = fast_state.shape[2]
    query_norm = rms_scaled(grouped[0].astype(jnp.float32)).astype(jnp.bfloat16)
    gathered = lax.all_gather(grouped[1:3], "seq", axis=1, tiled=True)
    rates = lax.all_gather(token_rate, "seq", axis=0, tiled=True)
    key_norm = rms_scaled(gathered[0].astype(jnp.float32)).astype(jnp.bfloat16)
    signal = (-rates * gathered[1].astype(jnp.float32)).astype(jnp.bfloat16)
    old_state = fast_state[:, 0]
    old_low = old_state.astype(jnp.bfloat16)
    old_full = lax.all_gather(old_low, "seq", axis=1, tiled=True)
    own_rows = row_gradient(key_norm, signal, old_low)
    summed = lax.all_gather(own_rows.astype(jnp.bfloat16), "seq", axis=1, tiled=True)
    direction = head_rate[0] * newton_schulz(summed.astype(jnp.float32))
    new_rows = old_state - lax.dynamic_slice_in_dim(
        direction, seq_index * state_rows, state_rows, 1
    )
    weight_piece = (old_full.astype(jnp.float32) - direction).astype(jnp.bfloat16)
    gate_act = contract_last(query_norm, weight_piece[0])
    up_act = contract_last(query_norm, weight_piece[1])
    active = (jax.nn.silu(gate_act) * up_act).astype(jnp.bfloat16)
    fast_out = jnp.dot(active, weight_piece[2], preferred_element_type=jnp.float32)
    span = WINDOW + tok_rows
    padded = jnp.pad(gathered, ((0, 0), (WINDOW, 0), (0, 0)))
    context = lax.dynamic_slice_in_dim(padded, seq_index * tok_rows, span, 1)
    scores = contract_last(grouped[0], context[0]) * head_dim ** (-0.5)
    query_pos = seq_index * tok_rows + jnp.arange(tok_rows, dtype=jnp.int32)[:, None]
    key_pos = (
        seq_index * tok_rows - WINDOW + jnp.arange(WINDOW + tok_rows, dtype=jnp.int32)[None, :]
    )
    visible = (key_pos <= query_pos) & (key_pos > query_pos - WINDOW) & (key_pos >= 0)
    scores = jnp.where(visible, scores, -jnp.inf)
    row_max = jnp.max(scores, axis=1, keepdims=True)
    exp_scores = jnp.exp(scores - row_max)
    weights = (exp_scores / jnp.sum(exp_scores, axis=1, keepdims=True)).astype(jnp.bfloat16)
    attention = jnp.dot(weights, context[1], preferred_element_type=jnp.float32)
    combined = (attention + fast_out).astype(jnp.bfloat16)
    tokens_back = lax.all_to_all(combined, "head", split_axis=0, concat_axis=1, tiled=True)
    return (tokens_back, new_rows[:, None])


def solution(mesh):
    return jax.shard_map(
        shards,
        mesh=mesh,
        in_specs=(
            P(None, ("seq", "head"), None),
            P("seq", "head"),
            P("head"),
            P(None, "head", "seq", None),
        ),
        out_specs=(P(("seq", "head"), None), P(None, "head", "seq", None)),
        check_vma=False,
    )
```

time: 290 us -> 193 us (0.67)
  the two profiles are of different devices: /device:TPU:16 before, /device:TPU:0 now
where the time goes in v1:
time: 193 us; the launch traced here: 192 us
  waiting for transfers between devices  88.7 us (46%)
  matrix products  41 us (21%)
  blocking collectives  32.4 us (17%)
  between operations  14.6 us (8%)
  other arithmetic  6.86 us (4%)
  local copies, waits for them, and re-layouts  4.98 us (3%)
  starting transfers between devices  3.68 us (2%)
    all_gather x1, waiting for transfers between devices, shards(): lax.all_gather(own_rows.astype(jnp.bfloat16), 'seq', axis=1, tiled=True)  35 us
    all_gather x1, waiting for transfers between devices, shards(): gathered = lax.all_gather(grouped[1:3], 'seq', axis=1, tiled=True)  29.1 us
    dot_general x4, matrix products, low_dot(): jnp.einsum(subscripts, left_side.astype(jnp.bfloat16), right_side.astype(...  28.5 us
    all_gather x1, blocking collectives, shards(): rates = lax.all_gather(token_rate, 'seq', axis=0, tiled=True)  21.8 us
    all_gather x1, waiting for transfers between devices, shards(): old_full = lax.all_gather(old_low, 'seq', axis=1, tiled=True)  21.2 us
    all_to_all x1, blocking collectives, shards(): lax.all_to_all(qkv, 'head', split_axis=2, concat_axis=1, tiled=True)  10.6 us
    dot_general x5, matrix products, contract_last(): lax.dot_general(left_side, right_side, (((1,), (1,)), ((), ())), preferre...  6.86 us
  transfers between devices with their start and end apart: 4, of which 4 were waited for; matrix products, arithmetic and copies ran while one was open for 12% of the time, Pallas kernels for 0%

profile of v1, /device:TPU:0, one launch (start us, length us, event | category | flops | bytes accessed | tf_op | source)
XLA Modules:
  0.0 192.2 jit_solution(13813779145525981337)
XLA Ops:
  7.2 0.0 all-gather.4.cloned.1.call-start
  7.2 1.6 copy.22
  8.8 0.0 copy-start.4
  8.8 0.0 copy-start.2
  8.8 0.8 reshape.99
  9.6 10.6 %all_to_all.34 = bf16[2,2,49152]{2,1,0:T(2,128)(2,1)S(1)} all-to-all(bf16[2,2,49152]{2,1,0:T(2,128)(2,1)S(1)} %reshape.99), channel_id=1, replica_groups=mesh['seq'=16,'head'=2] {'head'}, dimensions={0} | all-to-all | bytes 786432 | tf_op jit(solution)/shard_map/all_to_all | solution.py:73
  20.2 0.6 reshape.100
  20.8 0.6 copy.24
  21.4 0.7 slice.54
  22.1 0.0 all-gather.4.cloned.1.call-update
  22.2 0.0 all-gather.8.cloned.1.call-start
  22.2 0.0 copy-done.4
  22.2 21.8 %all_gather.14 = f32[2048,1]{0,1:T(1,128)S(1)} all-gather(f32[128,1]{0,1:T(1,128)S(1)} %copy-done.4), channel_id=1, replica_groups=mesh['seq'=16,'head'=2] {'seq'}, dimensions={0}, use_global_device_ids=true | all-gather | bytes 8704 | tf_op jit(solution)/shard_map/all_gather | solution.py:80
  44.0 0.0 copy-done.2
  44.0 0.0 copy-start.3
  44.1 29.1 %all-gather.4.cloned.1.call-done = bf16[2,2048,512]{2,1,0:T(8,128)(2,1)} async-done(((bf16[2,128,512]{2,1,0:T(8,128)(2,1)}), bf16[2,2048,512]{2,1,0:T(8,128)(2,1)}) %all-gather.4.cloned.1.call-update) | async-done | bytes 4194320 | tf_op jit(solution)/shard_map/all_gather | solution.py:79
  73.2 0.0 copy-start
  73.2 2.2 %fusion.5 = f32[2048]{0:T(1024)S(1)} fusion(bf16[2,2048,512]{2,1,0:T(8,128)(2,1)} %all-gather.4.cloned.1.call-done), kind=kLoop, calls=%fused_computation.11 | loop fusion | flops 3143680 | bytes 2105344 | tf_op jit(solution)/shard_map/reduce_sum | solution.py:18
  75.4 2.4 %fusion.52 = f32[2048,32]{0,1:T(8,128)S(1)} fusion(f32[2048]{0:T(1024)S(1)} %add_rsqrt_fusion, bf16[2,2048,512]{2,1,0:T(8,128)(2,1)} %all-gather.4.cloned.1.call-done, bf16[3,32,512]{2,1,0:T(8,128)(2,1)S(1)} %bitcast_convert_fusion), kind=kOutput, calls=%fused_computation.53 | convolution fusion | flops 70254592 | bytes 2400256 | tf_op jit(solution)/shard_map/dot_general | solution.py:22
  77.8 0.0 copy-done
  77.8 0.8 fusion.54
  78.6 0.0 copy-done.3
  78.7 0.8 fusion.15
  79.5 0.7 fusion.41
  80.2 0.7 fusion.40
  80.8 0.6 fusion.42
  81.5 0.7 pad_maximum_fusion
  82.1 0.0 all-gather.8.cloned.1.call-update
  82.2 0.2 all-gather.6.cloned.1.call-start
  82.4 0.5 all-gather.6.cloned.1.call-update
  83.6 0.1 fusion.62
  83.7 0.1 fusion.63
  83.8 1.5 fusion.92
  85.3 0.2 fusion.59
  85.5 35.0 %all-gather.8.cloned.1.call-done = bf16[3,512,512]{2,1,0:T(8,128)(2,1)} async-done(((bf16[3,32,512]{2,1,0:T(8,128)(2,1)}), bf16[3,512,512]{2,1,0:T(8,128)(2,1)}) %all-gather.8.cloned.1.call-update) | async-done | bytes 1572880 | tf_op jit(solution)/shard_map/all_gather | solution.py:87
  120.5 1.9 fusion.8
  122.4 0.0 copy-start.1
  122.4 4.8 %fusion.88 = f32[3,512,512]{2,1,0:T(8,128)} fusion(bf16[3,512,512]{2,1,0:T(8,128)(2,1)} %all-gather.8.cloned.1.call-done, f32[3]{0:T(128)S(1)} %sqrt_add_fusion), kind=kOutput, calls=%fused_computation.106 | convolution fusion | flops 807665664 | bytes 4718604 | tf_op jit(solution)/shard_map/mij,mkj->mik/dot_general | solution.py:54
  127.2 0.0 copy-done.1
  127.2 7.6 %multiply_add_fusion = f32[3,512,512]{2,1,0:T(8,128)} fusion(bf16[3,512,512]{2,1,0:T(8,128)(2,1)S(1)} %copy-done.1, f32[3]{0:T(128)S(1)} %sqrt_add_fusion, f32[3,512,512]{2,1,0:T(8,128)} %fusion.88), kind=kOutput, calls=%fused_computation.21 | convolution fusion | flops 1620049920 | bytes 7864332 | tf_op jit(solution)/shard_map/mij,mjk->mik/dot_general | solution.py:54
  134.8 5.6 %fusion.50 = f32[3,512,512]{2,1,0:T(8,128)} fusion(f32[3,512,512]{2,1,0:T(8,128)} %multiply_add_fusion), kind=kOutput, calls=%fused_computation.51 | convolution fusion | flops 806092800 | bytes 6291456 | tf_op jit(solution)/shard_map/mij,mkj->mik/dot_general | solution.py:54
  140.4 21.2 %all-gather.6.cloned.1.call-done = bf16[3,512,512]{2,1,0:T(8,128)(2,1)} async-done(((bf16[3,32,512]{2,1,0:T(8,128)(2,1)}), bf16[3,512,512]{2,1,0:T(8,128)(2,1)}) %all-gather.6.cloned.1.call-update) | async-done | bytes 1572880 | tf_op jit(solution)/shard_map/all_gather | solution.py:85
  161.6 10.5 %subtract_convert_fusion = (bf16[3,512,512]{2,1,0:T(8,128)(2,1)}, f32[3,512,512]{2,1,0:T(8,128)}) fusion(bf16[3,512,512]{2,1,0:T(8,128)(2,1)} %all-gather.6.cloned.1.call-done, f32[3,512,512]{2,1,0:T(8,128)} %multiply_add_fusion, f32[3,512,512]{2,1,0:T(8,128)} %fusion.50, f32[]{:T(128)} %bitcast.96), kind=kOutput, calls=%fused_computation.17 | convolution fusion | flops 1620049920 | bytes 12582916 | tf_op jit(solution)/shard_map/mij,mjk->mik/dot_general | solution.py:54
  172.1 1.3 fusion.58
  173.5 1.7 fusion.36
  175.1 2.0 %fusion.33 = bf16[128,512]{1,0:T(8,128)(2,1)} fusion(f32[128,512]{1,0:T(8,128)S(1)} %fusion.36, s32[]{:T(128)S(6)} %add.117, s32[]{:T(128)S(6)} %select_n.10, bf16[2,2048,512]{2,1,0:T(8,128)(2,1)} %all-gather.4.cloned.1.call-done, f32[128,1152]{0,1:T(8,128)S(1)} %get-tuple-element.15, f32[128]{0:T(128)S(1)} %fusion.59, f32[128]{0:T(128)S(1)} %get-tuple-element.14), kind=kOutput, calls=%fused_computation.42 | convolution fusion | flops 151568384 | bytes 5178376 | tf_op jit(solution)/shard_map/dot_general | solution.py:110
  177.1 3.4 %all-to-all-start.1 = ((bf16[2,64,512]{2,1,0:T(8,128)(2,1)}), bf16[2,64,512]{2,1,0:T(8,128)(2,1)S(1)}, u32[]{:S(2)}, u32[]{:S(2)}) async-start(bf16[2,64,512]{2,1,0:T(8,128)(2,1)} %bitcast.24), calls=%async_computation.1 | async-start | bytes 262144 | tf_op jit(solution)/shard_map/all_to_all | solution.py:112
  180.5 1.6 fusion.70
  182.1 2.8 %all-to-all-done.1 = bf16[2,64,512]{2,1,0:T(8,128)(2,1)S(1)} async-done(((bf16[2,64,512]{2,1,0:T(8,128)(2,1)}), bf16[2,64,512]{2,1,0:T(8,128)(2,1)S(1)}, u32[]{:S(2)}, u32[]{:S(2)}) %all-to-all-start.1) | async-done | bytes 131104 | tf_op jit(solution)/shard_map/all_to_all | solution.py:112
  185.0 0.7 copy.29
  (9 shorter events, 0.1 us)
Async XLA Ops:
  7.2 66.0 %all-gather.4.cloned.1.call-start = ((), (), s32[]{:S(2)}) async-start(), calls=%async_computation.2 | async-start | bytes 4456448 | tf_op jit(solution)/shard_map/all_gather | solution.py:79
  8.8 13.4 %copy-start.4 = (f32[128,1]{0,1:T(1,128)S(1)}, f32[128,1]{0,1:T(1,128)}, u32[]{:S(2)}) copy-start(f32[128,1]{0,1:T(1,128)} %param.5) | copy-start | bytes 1540
  8.8 35.2 %copy-start.2 = (f32[3,1,32,512]{3,2,1,0:T(8,128)S(1)}, f32[3,1,32,512]{3,2,1,0:T(8,128)}, u32[]{:S(2)}) copy-start(f32[3,1,32,512]{3,2,1,0:T(8,128)} %param.7) | copy-start | bytes 589828
  22.2 98.3 %all-gather.8.cloned.1.call-start = ((), (), s32[]{:S(2)}) async-start(), calls=%async_computation.4 | async-start | bytes 1671168 | tf_op jit(solution)/shard_map/all_gather | solution.py:87
  44.0 34.6 %copy-start.3 = (bf16[3,32,512]{2,1,0:T(8,128)(2,1)}, bf16[3,32,512]{2,1,0:T(8,128)(2,1)S(1)}, u32[]{:S(2)}) copy-start(bf16[3,32,512]{2,1,0:T(8,128)(2,1)S(1)} %bitcast_convert_fusion) | copy-start | bytes 294916
  73.2 4.6 %copy-start = (bf16[2,2048,512]{2,1,0:T(8,128)(2,1)S(1)}, bf16[2,2048,512]{2,1,0:T(8,128)(2,1)}, u32[]{:S(2)}) copy-start(bf16[2,2048,512]{2,1,0:T(8,128)(2,1)} %all-gather.4.cloned.1.call-done) | copy-start | bytes 12582916
  82.2 79.4 %all-gather.6.cloned.1.call-start = ((), (), s32[]{:S(2)}) async-start(), calls=%async_computation.3 | async-start | bytes 1671168 | tf_op jit(solution)/shard_map/all_gather | solution.py:85
  122.4 4.8 %copy-start.1 = (bf16[3,512,512]{2,1,0:T(8,128)(2,1)S(1)}, bf16[3,512,512]{2,1,0:T(8,128)(2,1)}, u32[]{:S(2)}) copy-start(bf16[3,512,512]{2,1,0:T(8,128)(2,1)} %all-gather.8.cloned.1.call-done) | copy-start | bytes 4718596
  177.1 7.9 %all-to-all-start.1 = ((bf16[2,64,512]{2,1,0:T(8,128)(2,1)}), bf16[2,64,512]{2,1,0:T(8,128)(2,1)S(1)}, u32[]{:S(2)}, u32[]{:S(2)}) async-start(bf16[2,64,512]{2,1,0:T(8,128)(2,1)} %bitcast.24), calls=%async_computation.1 | async-start | bytes 262144 | tf_op jit(solution)/shard_map/all_to_all | solution.py:112
Sparse Core Ops, SparseCore 0:
  22.3 50.8 all-gather.3
  82.3 38.1 all-gather.7
  123.2 38.3 all-gather.5

commit v2 on v1

v2 whole, which is shorter than its diff:
```python
import functools

import jax
import jax.numpy as jnp
from jax import lax
from jax.experimental import pallas as pl
from jax.experimental.pallas import tpu as pltpu
from jax.sharding import PartitionSpec as P

WINDOW = 1024
NS_STEPS = 2
MESH = pl.DeviceIdType.MESH

ns_first = 3.4445
ns_second = -4.775
ns_third = 2.0315
rms_eps = 1e-06
norm_eps = 1e-07

BF = jnp.bfloat16
F32 = jnp.float32


def rms_scaled(values):
    return values * lax.rsqrt(jnp.mean(values * values, axis=-1, keepdims=True) + rms_eps)


def dot_nt(left, right):
    return lax.dot_general(left, right, (((1,), (1,)), ((), ())), preferred_element_type=F32)


def dot_nn(left, right):
    return lax.dot_general(left, right, (((1,), (0,)), ((), ())), preferred_element_type=F32)


def kernel(
    S, H, wire,
    qkv_ref, rate_ref, hr_ref, state_ref,
    out_ref, new_ref,
    qbuf, kbuf, vbuf, rbuf, wbuf, gbuf, scores, acc_a, acc_b, attn, comb, xbuf,
    x_send, x_recv, o_send, o_recv, loc,
    r_send, r_recv, l_send, l_recv, p_send, p_recv,
):
    C = S // 2
    half = C // 2
    tok_rows, hd = qbuf.shape
    blk = tok_rows // H
    rows = state_ref.shape[1]
    fh = S * rows
    s = lax.axis_index("seq")
    h = lax.axis_index("head")
    chip, core = s // 2, s % 2
    row_y, row_z = chip % 2, chip // 2
    pos = (1 - row_y) * row_z + row_y * (C - 1 - row_z)

    def seq_of(q, which):
        far = q // half
        return 2 * ((1 - far) * (2 * q) + far * (2 * (C - 1 - q) + 1)) + which

    right = seq_of((pos + 1) % C, core)
    left = seq_of((pos + C - 1) % C, core)
    partner = chip * 2 + 1 - core
    others = [(h + j) % H for j in range(1, H)]

    barrier = pltpu.get_barrier_semaphore()
    for target in (right, left, partner):
        pl.semaphore_signal(barrier, inc=1, device_id=(target, h), device_id_type=MESH)
    for o in others:
        pl.semaphore_signal(barrier, inc=1, device_id=(s, o), device_id_type=MESH)
    wbuf[:, 0] = state_ref[...].astype(wire)
    rbuf[0] = rate_ref[...]
    pl.semaphore_wait(barrier, 3 + H - 1)

    def mine(o):
        return pl.ds(pl.multiple_of(o * blk, blk), blk)

    def cols(o):
        return pl.ds(pl.multiple_of(o * hd, hd), hd)

    parts = [(1, lambda: kbuf.at[0]), (2, lambda: vbuf.at[0]), (0, lambda: qbuf)]
    entry, local = {}, {}
    for which, dst in parts:
        for j, o in enumerate(others):
            entry[which, j] = pltpu.make_async_remote_copy(
                src_ref=qkv_ref.at[which, :, cols(o)],
                dst_ref=dst().at[mine(h)],
                send_sem=x_send.at[which, j], recv_sem=x_recv.at[which, j],
                device_id=(s, o), device_id_type=MESH,
            )
            entry[which, j].start()
        local[which] = pltpu.make_async_copy(
            qkv_ref.at[which, :, cols(h)], dst().at[mine(h)], loc.at[which]
        )
        local[which].start()

    up, down = half, C - 1 - half
    items = {
        "w": (0, lambda i: wbuf.at[:, i], down, up),
        "k": (1, lambda i: kbuf.at[i], up, down),
        "v": (2, lambda i: vbuf.at[i], down, up),
        "r": (3, lambda i: rbuf.at[i], up, down),
        "g0": (4, lambda i: gbuf.at[0, i], up, down),
        "g1": (5, lambda i: gbuf.at[1, i], down, up),
        "g2": (6, lambda i: gbuf.at[2, i], up, down),
    }
    sends = []
    pending = {}

    def remote(src, dst, ss, rs, target):
        copy = pltpu.make_async_remote_copy(
            src_ref=src, dst_ref=dst, send_sem=ss, recv_sem=rs,
            device_id=(target, h), device_id_type=MESH,
        )
        copy.start()
        sends.append(copy)
        return copy

    def to_partner(name, d):
        n, at, _, _ = items[name]
        pending["p", name, d] = remote(
            at(d), at(C + d), p_send.at[n, d], p_recv.at[n, d], partner
        )

    def ring(name, t):
        n, at, nr, nl = items[name]
        if 0 < t <= nr:
            pending["r", name, t - 1].wait_recv()
        if t < nr:
            pending["r", name, t] = remote(
                at((C - t) % C), at(C - t - 1), r_send.at[n, t], r_recv.at[n, t], right
            )
        if 0 < t <= nl:
            pending["l", name, t - 1].wait_recv()
        if t < nl:
            pending["l", name, t] = remote(
                at(t), at(t + 1), l_send.at[n, t], l_recv.at[n, t], left
            )
        if t == 0:
            to_partner(name, 0)
        if 0 < t <= nr:
            to_partner(name, C - t)
        if 0 < t <= nl:
            to_partner(name, t)

    def from_partner(name, d):
        pending["p", name, d].wait_recv()

    q_pos = s * tok_rows + lax.broadcasted_iota(jnp.int32, (tok_rows, tok_rows), 0)
    k_iota = lax.broadcasted_iota(jnp.int32, (tok_rows, tok_rows), 1)
    w_low = state_ref[...].astype(BF)
    w_gate_up = w_low[0:2].reshape(2 * rows, hd)
    w_down = w_low[2]
    acc_a[...] = jnp.zeros_like(acc_a)
    acc_b[...] = jnp.zeros_like(acc_b)

    def process(slot, origin):
        keys = kbuf[slot]
        values = vbuf[slot]
        key_norm = rms_scaled(keys.astype(F32)).astype(BF)
        neg_rate = -rbuf[slot]
        gate_up = dot_nt(w_gate_up, key_norm)
        gate, up_act = gate_up[:rows], gate_up[rows:]
        back = dot_nt(w_down, values) * neg_rate
        sig = jax.nn.sigmoid(gate)
        silu = gate * sig
        grad_gate = back * up_act * sig * (1.0 + gate * (1.0 - sig))
        grad_up = back * silu
        both = jnp.concatenate([grad_gate, grad_up], axis=0).astype(BF)
        acc_a[...] += dot_nn(both, key_norm)
        acc_b[...] += dot_nn((silu * up_act * neg_rate).astype(BF), values)
        sc = dot_nt(qbuf[...], keys) * hd ** (-0.5)
        k_pos = origin * tok_rows + k_iota
        visible = (k_pos <= q_pos) & (k_pos > q_pos - WINDOW)
        scores[:, slot * tok_rows:(slot + 1) * tok_rows] = jnp.where(visible, sc, -jnp.inf)

    def process_own(d):
        process(d, seq_of((pos + d) % C, core))

    def process_partner(d):
        for name in ("k", "v", "r"):
            from_partner(name, d)
        process(C + d, seq_of((pos + d) % C, 1 - core))

    ring("w", 0)
    for which in (1, 2):
        local[which].wait()
        for j in range(H - 1):
            entry[which, j].wait_recv()
    for name in ("k", "v", "r"):
        ring(name, 0)
    local[0].wait()
    for j in range(H - 1):
        entry[0, j].wait_recv()
    ring_slots = [[0]]
    for t in range(1, half + 1):
        ring_slots.append(sorted({C - t, t}))
    for t in range(half + 1):
        if t > 0:
            for name in ("w", "k", "v", "r"):
                ring(name, t)
        if t > 0:
            for d in ring_slots[t - 1]:
                process_partner(d)
        for d in ring_slots[t]:
            process_own(d)
    for d in ring_slots[half]:
        process_partner(d)

    gbuf[0, 0] = acc_a[:rows].astype(wire)
    gbuf[1, 0] = acc_a[rows:].astype(wire)
    gbuf[2, 0] = acc_b[...].astype(wire)
    grads = ("g0", "g1", "g2")
    for name in grads:
        ring(name, 0)
    row_max = jnp.max(scores[...], axis=1, keepdims=True)
    scores[...] = jnp.exp(scores[...] - row_max)
    for t in range(1, half + 1):
        for name in grads:
            ring(name, t)
        if t == 1:
            total = jnp.sum(scores[...], axis=1, keepdims=True)
            weights = (scores[...] / total).astype(BF)
            attn[...] = dot_nn(weights, vbuf[...].reshape(S * tok_rows, hd))
    for d in range(C):
        from_partner("w", d)
        for name in grads:
            from_partner(name, d)
    for copy in sends:
        copy.wait_send()
    for copy in entry.values():
        copy.wait_send()

    rate = hr_ref[0]

    def update(m, carry):
        grad = gbuf[m].reshape(fh, hd).astype(F32)
        frob = jnp.sqrt(jnp.sum(grad * grad, keepdims=True))
        xbuf[...] = grad / (frob + norm_eps)
        for _ in range(NS_STEPS):
            low = xbuf[...].astype(BF)
            gram = dot_nt(low, low)
            gram_low = gram.astype(BF)
            poly = ns_second * gram + ns_third * dot_nn(gram_low, gram_low)
            xbuf[...] = ns_first * xbuf[...] + dot_nn(poly.astype(BF), low)
        new_ref[m] = state_ref[m] - rate * xbuf[0:rows]
        fresh = wbuf[m].reshape(fh, hd).astype(F32) - rate * xbuf[...]
        wbuf[m] = fresh.astype(wire).reshape(S, rows, hd)
        return carry

    lax.fori_loop(0, 3, update, 0)

    query_norm = rms_scaled(qbuf[...].astype(F32)).astype(BF)
    gate_q = dot_nt(query_norm, wbuf[0].reshape(fh, hd).astype(BF))
    up_q = dot_nt(query_norm, wbuf[1].reshape(fh, hd).astype(BF))
    active_q = (jax.nn.silu(gate_q) * up_q).astype(BF)
    fast_out = dot_nn(active_q, wbuf[2].reshape(fh, hd).astype(BF))
    comb[...] = (attn[...] + fast_out).astype(BF)
    back_copies = []
    for j, o in enumerate(others):
        copy = pltpu.make_async_remote_copy(
            src_ref=comb.at[mine(o)], dst_ref=out_ref.at[:, cols(h)],
            send_sem=o_send.at[j], recv_sem=o_recv.at[j],
            device_id=(s, o), device_id_type=MESH,
        )
        copy.start()
        back_copies.append(copy)
    own = pltpu.make_async_copy(comb.at[mine(h)], out_ref.at[:, cols(h)], loc.at[3])
    own.start()
    own.wait()
    for copy in back_copies:
        copy.wait()


def shards(S, H, qkv, token_rate, head_rate, fast_state):
    hd = qkv.shape[2] // H
    blk = qkv.shape[1]
    tok_rows = blk * H
    rows = fast_state.shape[2]
    wire = BF if rows % 16 == 0 else F32
    C = S // 2
    half = max(C // 2, 1)
    dma = pltpu.SemaphoreType.DMA
    vmem = pl.BlockSpec(memory_space=pltpu.VMEM)
    out, new_rows = pl.pallas_call(
        functools.partial(kernel, S, H, wire),
        out_shape=(
            jax.ShapeDtypeStruct((blk, H * hd), BF),
            jax.ShapeDtypeStruct((3, rows, hd), F32),
        ),
        in_specs=[vmem, vmem, pl.BlockSpec(memory_space=pltpu.SMEM), vmem],
        out_specs=(vmem, vmem),
        scratch_shapes=[
            pltpu.VMEM((tok_rows, hd), BF),
            pltpu.VMEM((S, tok_rows, hd), BF),
            pltpu.VMEM((S, tok_rows, hd), BF),
            pltpu.VMEM((S, 1, tok_rows), F32),
            pltpu.VMEM((3, S, rows, hd), wire),
            pltpu.VMEM((3, S, rows, hd), wire),
            pltpu.VMEM((tok_rows, S * tok_rows), F32),
            pltpu.VMEM((2 * rows, hd), F32),
            pltpu.VMEM((rows, hd), F32),
            pltpu.VMEM((tok_rows, hd), F32),
            pltpu.VMEM((tok_rows, hd), BF),
            pltpu.VMEM((S * rows, hd), F32),
            dma((3, max(H - 1, 1))), dma((3, max(H - 1, 1))),
            dma((max(H - 1, 1),)), dma((max(H - 1, 1),)), dma((4,)),
            dma((7, half)), dma((7, half)), dma((7, half)), dma((7, half)),
            dma((7, C)), dma((7, C)),
        ],
        compiler_params=pltpu.CompilerParams(collective_id=0, has_side_effects=True),
    )(qkv, token_rate.reshape(1, tok_rows), head_rate, fast_state[:, 0])
    return (out, new_rows[:, None])


def solution(mesh):
    return jax.shard_map(
        functools.partial(shards, mesh.shape["seq"], mesh.shape["head"]),
        mesh=mesh,
        in_specs=(
            P(None, ("seq", "head"), None),
            P("seq", "head"),
            P("head"),
            P(None, "head", "seq", None),
        ),
        out_specs=(P(("seq", "head"), None), P(None, "head", "seq", None)),
        check_vma=False,
    )
```

time: 193 us -> 73.1 us (0.38)
  waiting for transfers between devices: 88.7 us -> 0 us
  Pallas kernels: 0 us -> 69.3 us
  matrix products: 41 us -> 0 us
  blocking collectives: 32.4 us -> 0 us
  between operations: 14.6 us -> 1.29 us
  other arithmetic: 6.86 us -> 0 us
  starting transfers between devices: 3.68 us -> 0 us
  local copies, waits for them, and re-layouts: 4.98 us -> 2.29 us
    all_gather x3 -> x0, waiting for transfers between devices: 85.3 us -> none  [the longest x1 35 us: shards(): lax.all_gather(own_rows.astype(jnp.bfloat16), 'seq', axis=1, tiled=True)]
    pallas_call x0 -> x1, Pallas kernels: none -> 69.3 us  [shards(): pl.pallas_call(functools.partial(kernel, S, H, wire), out_shape=(jax.Shap...]
    dot_general x14 -> x0, matrix products: 41 us -> none  [the longest x4 28.5 us: low_dot(): jnp.einsum(subscripts, left_side.astype(jnp.bfloat16), right_side.astype(...]
    all_gather x1 -> x0, blocking collectives: 21.8 us -> none  [shards(): rates = lax.all_gather(token_rate, 'seq', axis=0, tiled=True)]
    all_to_all x1 -> x0, blocking collectives: 10.6 us -> none  [shards(): lax.all_to_all(qkv, 'head', split_axis=2, concat_axis=1, tiled=True)]
    reduce_sum x4 -> x0, other arithmetic: 4.4 us -> none  [the longest x2 2.33 us: rms_scaled(): jnp.mean(values * values, axis=-1, keepdims=True) + rms_eps]
    all_to_all x1 -> x0, starting transfers between devices: 3.38 us -> none  [shards(): lax.all_to_all(combined, 'head', split_axis=0, concat_axis=1, tiled=True)]
    all_to_all x1 -> x0, waiting for transfers between devices: 2.83 us -> none  [shards(): lax.all_to_all(combined, 'head', split_axis=0, concat_axis=1, tiled=True)]
  transfers between devices with their start and end apart: 4 -> 0, of which waited for: 4 -> 0; matrix products, arithmetic and copies ran while one was open for 12% -> 0% of each run, Pallas kernels for 0% -> 0%
where the time goes in v2:
time: 73.1 us; the launch traced here: 72.9 us
  Pallas kernels  69.3 us (95%)
  local copies, waits for them, and re-layouts  2.29 us (3%)
  between operations  1.29 us (2%)
    pallas_call x1, Pallas kernels, shards(): pl.pallas_call(functools.partial(kernel, S, H, wire), out_shape=(jax.Shap...  69.3 us
    unnamed x4, local copies, waits for them, and re-layouts  2.29 us

profile of v2, /device:TPU:0, one launch (start us, length us, event | category | flops | bytes accessed | tf_op | source)
XLA Modules:
  0.0 72.9 jit_solution(1738976226701265142)
XLA Ops:
  1.3 69.3 %shard_map.59 = (bf16[64,1024]{1,0:T(8,128)(2,1)}, f32[3,32,512]{2,1,0:T(8,128)}) custom-call(bf16[3,64,1024]{2,1,0:T(8,128)(2,1)} %qkv_ref.1, f32[1,128]{1,0:T(1,128)} %bitcast.7, f32[1]{0:T(128)S(6)} %copy.9.hr_ref, f32[3,32,512]{2,1,0:T(8,128)} %bitcast.6), custom_call_target="tpu_custom_call" | custom-call | tf_op jit(solution)/shard_map/pallas_call | solution.py:284
  70.6 0.0 copy-start
  70.6 1.6 %copy.10 = bf16[64,1024]{1,0:T(8,128)(2,1)} copy(bf16[64,1024]{1,0:T(8,128)(2,1)} %get-tuple-element.10) | data formatting | bytes 262144
  72.2 0.0 copy-done
  72.2 0.7 copy.11
Async XLA Ops:
  70.6 1.6 %copy-start = (f32[3,32,512]{2,1,0:T(8,128)S(1)}, f32[3,32,512]{2,1,0:T(8,128)}, u32[]{:S(2)}) copy-start(f32[3,32,512]{2,1,0:T(8,128)} %get-tuple-element.5) | copy-start | bytes 589828

commit v3 on v2

--- a/solution.py
+++ b/solution.py
@@ -94,15 +94,17 @@
         local[which].start()
 
     up, down = half, C - 1 - half
-    items = {
-        "w": (0, lambda i: wbuf.at[:, i], down, up),
-        "k": (1, lambda i: kbuf.at[i], up, down),
-        "v": (2, lambda i: vbuf.at[i], down, up),
-        "r": (3, lambda i: rbuf.at[i], up, down),
-        "g0": (4, lambda i: gbuf.at[0, i], up, down),
-        "g1": (5, lambda i: gbuf.at[1, i], down, up),
-        "g2": (6, lambda i: gbuf.at[2, i], up, down),
-    }
+    spans = [mine(h), mine(others[0])] if H == 2 else [slice(None)]
+    items = {"r": (0, lambda i: rbuf.at[i], up, down), "w": (1, lambda i: wbuf.at[:, i], down, up)}
+    for m in range(3):
+        lanes = (down, up) if m == 1 else (up, down)
+        items["g", m] = (2 + m, lambda i, m=m: gbuf.at[m, i], *lanes)
+    for j, span in enumerate(spans):
+        items["k", j] = (5 + 2 * j, lambda i, span=span: kbuf.at[i, span], up, down)
+        items["v", j] = (6 + 2 * j, lambda i, span=span: vbuf.at[i, span], down, up)
+    first = [("k", 0), ("v", 0), "r"]
+    second = [("k", j) for j in range(1, len(spans))] + [("v", j) for j in range(1, len(spans))]
+    grads = [("g", m) for m in range(3)]
     sends = []
     pending = {}
 
@@ -177,16 +179,20 @@
         process(d, seq_of((pos + d) % C, core))
 
     def process_partner(d):
-        for name in ("k", "v", "r"):
+        for name in first + second:
             from_partner(name, d)
         process(C + d, seq_of((pos + d) % C, 1 - core))
 
+    for which in (1, 2):
+        local[which].wait()
+    if H == 2:
+        for name in first:
+            ring(name, 0)
     ring("w", 0)
     for which in (1, 2):
-        local[which].wait()
         for j in range(H - 1):
             entry[which, j].wait_recv()
-    for name in ("k", "v", "r"):
+    for name in second if H == 2 else first:
         ring(name, 0)
     local[0].wait()
     for j in range(H - 1):
@@ -196,20 +202,24 @@
         ring_slots.append(sorted({C - t, t}))
     for t in range(half + 1):
         if t > 0:
-            for name in ("w", "k", "v", "r"):
+            for name in first + second:
                 ring(name, t)
+        if t == half - 1:
+            for late in range(1, half - 2):
+                ring("w", late)
         if t > 0:
             for d in ring_slots[t - 1]:
                 process_partner(d)
         for d in ring_slots[t]:
             process_own(d)
+        if t == half:
+            ring("w", half - 2)
     for d in ring_slots[half]:
         process_partner(d)
 
     gbuf[0, 0] = acc_a[:rows].astype(wire)
     gbuf[1, 0] = acc_a[rows:].astype(wire)
     gbuf[2, 0] = acc_b[...].astype(wire)
-    grads = ("g0", "g1", "g2")
     for name in grads:
         ring(name, 0)
     row_max = jnp.max(scores[...], axis=1, keepdims=True)
@@ -217,43 +227,45 @@
     for t in range(1, half + 1):
         for name in grads:
             ring(name, t)
+        if t == half - 1:
+            ring("w", half - 1)
         if t == 1:
             total = jnp.sum(scores[...], axis=1, keepdims=True)
             weights = (scores[...] / total).astype(BF)
             attn[...] = dot_nn(weights, vbuf[...].reshape(S * tok_rows, hd))
     for d in range(C):
-        from_partner("w", d)
         for name in grads:
             from_partner(name, d)
-    for copy in sends:
-        copy.wait_send()
-    for copy in entry.values():
-        copy.wait_send()
-
     rate = hr_ref[0]
 
-    def update(m, carry):
+    def orthogonal(m):
         grad = gbuf[m].reshape(fh, hd).astype(F32)
         frob = jnp.sqrt(jnp.sum(grad * grad, keepdims=True))
-        xbuf[...] = grad / (frob + norm_eps)
+        xbuf[m] = grad / (frob + norm_eps)
         for _ in range(NS_STEPS):
-            low = xbuf[...].astype(BF)
+            low = xbuf[m].astype(BF)
             gram = dot_nt(low, low)
             gram_low = gram.astype(BF)
             poly = ns_second * gram + ns_third * dot_nn(gram_low, gram_low)
-            xbuf[...] = ns_first * xbuf[...] + dot_nn(poly.astype(BF), low)
-        new_ref[m] = state_ref[m] - rate * xbuf[0:rows]
-        fresh = wbuf[m].reshape(fh, hd).astype(F32) - rate * xbuf[...]
-        wbuf[m] = fresh.astype(wire).reshape(S, rows, hd)
-        return carry
-
-    lax.fori_loop(0, 3, update, 0)
+            xbuf[m] = ns_first * xbuf[m] + dot_nn(poly.astype(BF), low)
+        new_ref[m] = state_ref[m] - rate * xbuf[m, 0:rows]
+
+    def fresh(m):
+        old = wbuf[m].reshape(fh, hd).astype(F32)
+        return (old - rate * xbuf[m]).astype(BF)
+
+    orthogonal(0)
+    ring("w", half)
+    orthogonal(1)
+    orthogonal(2)
+    for d in range(C):
+        from_partner("w", d)
 
     query_norm = rms_scaled(qbuf[...].astype(F32)).astype(BF)
-    gate_q = dot_nt(query_norm, wbuf[0].reshape(fh, hd).astype(BF))
-    up_q = dot_nt(query_norm, wbuf[1].reshape(fh, hd).astype(BF))
+    gate_q = dot_nt(query_norm, fresh(0))
+    up_q = dot_nt(query_norm, fresh(1))
     active_q = (jax.nn.silu(gate_q) * up_q).astype(BF)
-    fast_out = dot_nn(active_q, wbuf[2].reshape(fh, hd).astype(BF))
+    fast_out = dot_nn(active_q, fresh(2))
     comb[...] = (attn[...] + fast_out).astype(BF)
     back_copies = []
     for j, o in enumerate(others):
@@ -269,6 +281,10 @@
     own.wait()
     for copy in back_copies:
         copy.wait()
+    for copy in sends:
+        copy.wait_send()
+    for copy in entry.values():
+        copy.wait_send()
 
 
 def shards(S, H, qkv, token_rate, head_rate, fast_state):
@@ -301,11 +317,11 @@
             pltpu.VMEM((rows, hd), F32),
             pltpu.VMEM((tok_rows, hd), F32),
             pltpu.VMEM((tok_rows, hd), BF),
-            pltpu.VMEM((S * rows, hd), F32),
+            pltpu.VMEM((3, S * rows, hd), F32),
             dma((3, max(H - 1, 1))), dma((3, max(H - 1, 1))),
             dma((max(H - 1, 1),)), dma((max(H - 1, 1),)), dma((4,)),
-            dma((7, half)), dma((7, half)), dma((7, half)), dma((7, half)),
-            dma((7, C)), dma((7, C)),
+            dma((9, half)), dma((9, half)), dma((9, half)), dma((9, half)),
+            dma((9, C)), dma((9, C)),
         ],
         compiler_params=pltpu.CompilerParams(collective_id=0, has_side_effects=True),
     )(qkv, token_rate.reshape(1, tok_rows), head_rate, fast_state[:, 0])

time: 73.1 us -> 66 us (0.903)
  Pallas kernels: 69.3 us -> 62.3 us
    pallas_call x1, Pallas kernels: 69.3 us -> 62.3 us  [shards(): pl.pallas_call(functools.partial(kernel, S, H, wire), out_shape=(jax.Shap...]
where the time goes in v3:
time: 66 us; the launch traced here: 65.8 us
  Pallas kernels  62.3 us (94%)
  local copies, waits for them, and re-layouts  2.29 us (3%)
  between operations  1.29 us (2%)
    pallas_call x1, Pallas kernels, shards(): pl.pallas_call(functools.partial(kernel, S, H, wire), out_shape=(jax.Shap...  62.3 us
    unnamed x4, local copies, waits for them, and re-layouts  2.29 us

profile of v3, /device:TPU:0, one launch (start us, length us, event | category | flops | bytes accessed | tf_op | source)
XLA Modules:
  0.0 65.8 jit_solution(16273253761644775059)
XLA Ops:
  1.3 62.3 %shard_map.59 = (bf16[64,1024]{1,0:T(8,128)(2,1)}, f32[3,32,512]{2,1,0:T(8,128)}) custom-call(bf16[3,64,1024]{2,1,0:T(8,128)(2,1)} %qkv_ref.1, f32[1,128]{1,0:T(1,128)} %bitcast.7, f32[1]{0:T(128)S(6)} %copy.9.hr_ref, f32[3,32,512]{2,1,0:T(8,128)} %bitcast.6), custom_call_target="tpu_custom_call" | custom-call | tf_op jit(solution)/shard_map/pallas_call | solution.py:300
  63.5 0.0 copy-start
  63.5 1.6 %copy.10 = bf16[64,1024]{1,0:T(8,128)(2,1)} copy(bf16[64,1024]{1,0:T(8,128)(2,1)} %get-tuple-element.10) | data formatting | bytes 262144
  65.2 0.0 copy-done
  65.2 0.7 %copy.11 = f32[3,1,32,512]{3,2,1,0:T(8,128)} copy(f32[3,1,32,512]{3,2,1,0:T(8,128)S(1)} %bitcast.5) | data formatting | bytes 393216
Async XLA Ops:
  63.5 1.6 %copy-start = (f32[3,32,512]{2,1,0:T(8,128)S(1)}, f32[3,32,512]{2,1,0:T(8,128)}, u32[]{:S(2)}) copy-start(f32[3,32,512]{2,1,0:T(8,128)} %get-tuple-element.5) | copy-start | bytes 589828

commit v4 on v3

--- a/solution.py
+++ b/solution.py
@@ -201,19 +201,20 @@
     for t in range(1, half + 1):
         ring_slots.append(sorted({C - t, t}))
     for t in range(half + 1):
+        if t == half:
+            for d in ring_slots[t - 1]:
+                process_partner(d)
         if t > 0:
             for name in first + second:
                 ring(name, t)
         if t == half - 1:
             for late in range(1, half - 2):
                 ring("w", late)
-        if t > 0:
+        if 0 < t < half:
             for d in ring_slots[t - 1]:
                 process_partner(d)
         for d in ring_slots[t]:
             process_own(d)
-        if t == half:
-            ring("w", half - 2)
     for d in ring_slots[half]:
         process_partner(d)
 
@@ -227,7 +228,9 @@
     for t in range(1, half + 1):
         for name in grads:
             ring(name, t)
-        if t == half - 1:
+        if t == half - 2:
+            ring("w", half - 2)
+        if t == half:
             ring("w", half - 1)
         if t == 1:
             total = jnp.sum(scores[...], axis=1, keepdims=True)
@@ -255,8 +258,8 @@
         return (old - rate * xbuf[m]).astype(BF)
 
     orthogonal(0)
+    orthogonal(1)
     ring("w", half)
-    orthogonal(1)
     orthogonal(2)
     for d in range(C):
         from_partner("w", d)

time: 66 us -> 64.3 us (0.974)
  Pallas kernels: 62.3 us -> 60.6 us
    pallas_call x1, Pallas kernels: 62.3 us -> 60.6 us  [shards(): pl.pallas_call(functools.partial(kernel, S, H, wire), out_shape=(jax.Shap...]
where the time goes in v4:
time: 64.3 us; the launch traced here: 64.2 us
  Pallas kernels  60.6 us (94%)
  local copies, waits for them, and re-layouts  2.29 us (4%)
  between operations  1.29 us (2%)
    pallas_call x1, Pallas kernels, shards(): pl.pallas_call(functools.partial(kernel, S, H, wire), out_shape=(jax.Shap...  60.6 us
    unnamed x4, local copies, waits for them, and re-layouts  2.29 us

profile of v4, /device:TPU:0, one launch (start us, length us, event | category | flops | bytes accessed | tf_op | source)
XLA Modules:
  0.0 64.2 jit_solution(12892568128128308184)
XLA Ops:
  1.3 60.6 %shard_map.59 = (bf16[64,1024]{1,0:T(8,128)(2,1)}, f32[3,32,512]{2,1,0:T(8,128)}) custom-call(bf16[3,64,1024]{2,1,0:T(8,128)(2,1)} %qkv_ref.1, f32[1,128]{1,0:T(1,128)} %bitcast.7, f32[1]{0:T(128)S(6)} %copy.9.hr_ref, f32[3,32,512]{2,1,0:T(8,128)} %bitcast.6), custom_call_target="tpu_custom_call" | custom-call | tf_op jit(solution)/shard_map/pallas_call | solution.py:303
  61.9 0.0 copy-start
  61.9 1.6 %copy.10 = bf16[64,1024]{1,0:T(8,128)(2,1)} copy(bf16[64,1024]{1,0:T(8,128)(2,1)} %get-tuple-element.10) | data formatting | bytes 262144
  63.5 0.0 copy-done
  63.5 0.7 %copy.11 = f32[3,1,32,512]{3,2,1,0:T(8,128)} copy(f32[3,1,32,512]{3,2,1,0:T(8,128)S(1)} %bitcast.5) | data formatting | bytes 393216
Async XLA Ops:
  61.9 1.6 %copy-start = (f32[3,32,512]{2,1,0:T(8,128)S(1)}, f32[3,32,512]{2,1,0:T(8,128)}, u32[]{:S(2)}) copy-start(f32[3,32,512]{2,1,0:T(8,128)} %get-tuple-element.5) | copy-start | bytes 589828

commit v5 on v4

--- a/solution.py
+++ b/solution.py
@@ -236,12 +236,11 @@
             total = jnp.sum(scores[...], axis=1, keepdims=True)
             weights = (scores[...] / total).astype(BF)
             attn[...] = dot_nn(weights, vbuf[...].reshape(S * tok_rows, hd))
-    for d in range(C):
-        for name in grads:
-            from_partner(name, d)
     rate = hr_ref[0]
 
     def orthogonal(m):
+        for d in range(C):
+            from_partner(grads[m], d)
         grad = gbuf[m].reshape(fh, hd).astype(F32)
         frob = jnp.sqrt(jnp.sum(grad * grad, keepdims=True))
         xbuf[m] = grad / (frob + norm_eps)

time: 64.3 us -> 65.4 us (1.017)
  Pallas kernels: 60.6 us -> 61.7 us
    pallas_call x1, Pallas kernels: 60.6 us -> 61.7 us  [shards(): pl.pallas_call(functools.partial(kernel, S, H, wire), out_shape=(jax.Shap...]
where the time goes in v5:
time: 65.4 us; the launch traced here: 65.3 us
  Pallas kernels  61.7 us (94%)
  local copies, waits for them, and re-layouts  2.29 us (4%)
  between operations  1.29 us (2%)
    pallas_call x1, Pallas kernels, shards(): pl.pallas_call(functools.partial(kernel, S, H, wire), out_shape=(jax.Shap...  61.7 us
    unnamed x4, local copies, waits for them, and re-layouts  2.29 us

profile of v5, /device:TPU:0, one launch (start us, length us, event | category | flops | bytes accessed | tf_op | source)
XLA Modules:
  0.0 65.3 jit_solution(5428530584580568479)
XLA Ops:
  1.3 61.7 %shard_map.59 = (bf16[64,1024]{1,0:T(8,128)(2,1)}, f32[3,32,512]{2,1,0:T(8,128)}) custom-call(bf16[3,64,1024]{2,1,0:T(8,128)(2,1)} %qkv_ref.1, f32[1,128]{1,0:T(1,128)} %bitcast.7, f32[1]{0:T(128)S(6)} %copy.9.hr_ref, f32[3,32,512]{2,1,0:T(8,128)} %bitcast.6), custom_call_target="tpu_custom_call" | custom-call | tf_op jit(solution)/shard_map/pallas_call | solution.py:302
  63.0 0.0 copy-start
  63.0 1.6 %copy.10 = bf16[64,1024]{1,0:T(8,128)(2,1)} copy(bf16[64,1024]{1,0:T(8,128)(2,1)} %get-tuple-element.10) | data formatting | bytes 262144
  64.6 0.0 copy-done
  64.6 0.7 %copy.11 = f32[3,1,32,512]{3,2,1,0:T(8,128)} copy(f32[3,1,32,512]{3,2,1,0:T(8,128)S(1)} %bitcast.5) | data formatting | bytes 393216
Async XLA Ops:
  63.0 1.6 %copy-start = (f32[3,32,512]{2,1,0:T(8,128)S(1)}, f32[3,32,512]{2,1,0:T(8,128)}, u32[]{:S(2)}) copy-start(f32[3,32,512]{2,1,0:T(8,128)} %get-tuple-element.5) | copy-start | bytes 589828
